TPU v7x, 32 devices: a whole 2x2x4 slice. The times are simulated.
32 devices in a mesh: seq: 8 (over y, x, core), tp: 4 (over z).
Axes of the slice: x: 2, y: 2, z: 4, core: 2. Of those that a mesh axis runs over, the one named last changes fastest.
Arguments:
- tokens: bfloat16 [1, 4096, 2048], P(None, 'seq'), may hold values from -6 to 6
- gain_attn: float32 [2048], replicated, may hold values from 0.5 to 1.5
- w_query: bfloat16 [2048, 2048], P(None, 'tp'), may hold values from -0.21875 to 0.21875
- w_key: bfloat16 [2048, 2048], P(None, 'tp'), may hold values from -0.21875 to 0.21875
- w_value: bfloat16 [2048, 2048], P(None, 'tp'), may hold values from -0.125 to 0.125
- w_out: bfloat16 [2048, 2048], P('tp'), may hold values from -0.25 to 0.25
- gain_ffn: float32 [2048], replicated, may hold values from 0.5 to 1.5
- w_gate: bfloat16 [2048, 8192], P(None, 'tp'), may hold values from -0.125 to 0.125
- w_up: bfloat16 [2048, 8192], P(None, 'tp'), may hold values from -0.125 to 0.125
- w_down: bfloat16 [8192, 2048], P('tp'), may hold values from -0.0625 to 0.0625
- cotangent: bfloat16 [1, 4096, 2048], P(None, 'seq'), may hold values from -6 to 6
- doc_ids: int32 [1, 4096], replicated, may hold values from 0 to 15, never falling along the last dimension, each value on 1 to 2048 neighbouring positions
- valid: int32 [1, 4096], replicated, may hold values 0 or 1
- group_order: int32 [1, 16], replicated, may hold values from 0 to 15, each once within a row
Outputs:
- layer_out: bfloat16 [1, 4096, 2048], P(None, 'seq')
- grad_tokens: float32 [1, 4096, 2048], P(None, 'seq')
- grad_gain_attn: float32 [2048], P('seq')
- grad_query: float32 [2048, 2048], P('seq', 'tp')
- grad_key: float32 [2048, 2048], P('seq', 'tp')
- grad_value: float32 [2048, 2048], P('seq', 'tp')
- grad_out: float32 [2048, 2048], P('tp', 'seq')
- grad_gain_ffn: float32 [2048], P('seq')
- grad_gate: float32 [2048, 8192], P('seq', 'tp')
- grad_up: float32 [2048, 8192], P('seq', 'tp')
- grad_down: float32 [8192, 2048], P('tp', 'seq')
Inputs may be any that keep to these rules, and one draw needn't show every extreme that they name: `doc_ids`: document numbers never fall along a sequence; a document holds 1 to 2048 positions. `group_order`: each row is a permutation; device i of seq stores storage blocks 2 i and 2 i + 1 of every sequence.
All inputs are finite; a program needn't handle non-finite values.
Results may differ from a plain program's by a relative error of at most 0.014.
The roundings to bfloat16 on the way count: a program that leaves them out, or rounds other values in their place, can miss the bound.
Values may be sent and summed in bfloat16 or wider, within the bound.
No kernel may reach another device: no remote copies, remote signals or barrier semaphores. Data moves between devices by JAX's collectives and lax.ppermute only.
A program may use at most 320 MiB of HBM per device.

v0:
```python
import math
import jax
import jax.numpy as jnp
from jax import lax
from jax.sharding import PartitionSpec as P

HEAD_WIDTH = 128
norm_eps = 1e-05
rope_base = 10000.0


def rope_tables(places, head_size):
    half_size = head_size // 2
    freqs = rope_base ** (-jnp.arange(half_size, dtype=jnp.float32) * 2.0 / head_size)
    angles = places.astype(jnp.float32)[..., None] * freqs
    return (jnp.cos(angles), jnp.sin(angles))


def rotate(values, cosine, sine, forward):
    half_size = values.shape[-1] // 2
    first = values[..., :half_size]
    second = values[..., half_size:]
    cos_b = cosine[..., None, :]
    sin_b = sine[..., None, :]
    if forward:
        return jnp.concatenate(
            [first * cos_b - second * sin_b, second * cos_b + first * sin_b], axis=-1
        )
    return jnp.concatenate(
        [first * cos_b + second * sin_b, second * cos_b - first * sin_b], axis=-1
    )


def visible(place_q, doc_q, place_k, doc_k, live_k):
    allowed = (
        (place_k[None, :] <= place_q[:, None])
        & (doc_k[None, :] == doc_q[:, None])
        & (live_k[None, :] == 1)
    )
    return allowed.astype(jnp.float32)


def score_block(query_heads, key_heads, head_size, length):
    scores = jnp.einsum("qhe,khe->hqk", query_heads, key_heads, preferred_element_type=jnp.float32)
    return scores * (1.0 / math.sqrt(head_size)) - math.log(length)


def score_grads(query_heads, key_heads, value_heads, grad_heads, mask, head_size, length):
    sigma = jax.nn.sigmoid(score_block(query_heads, key_heads, head_size, length))
    weights = (sigma * mask).astype(jnp.bfloat16)
    grad_weights = jnp.einsum(
        "qhe,khe->hqk", grad_heads, value_heads, preferred_element_type=jnp.float32
    )
    grad_scores = (grad_weights * (sigma * (1.0 - sigma)) * mask).astype(jnp.bfloat16)
    return (weights, grad_scores)


def local(
    tokens,
    gain_attn,
    w_query,
    w_key,
    w_value,
    w_out,
    gain_ffn,
    w_gate,
    w_up,
    w_down,
    cotangent,
    doc_ids,
    valid,
    group_order,
):
    seq_count, row_count, model_width = tokens.shape
    length = doc_ids.shape[1]
    span = length // group_order.shape[1]
    head_size = HEAD_WIDTH
    local_width = w_query.shape[1]
    local_heads = local_width // head_size
    flat_rows = seq_count * row_count
    factor = 1.0 / math.sqrt(head_size)
    own_rows = lax.axis_index("seq") * row_count + jnp.arange(row_count, dtype=jnp.int32)
    all_rows = jnp.arange(length, dtype=jnp.int32)
    place_all = jnp.take(group_order, all_rows // span, axis=1) * span + (all_rows % span)[None, :]
    place_own = jnp.take(group_order, own_rows // span, axis=1) * span + (own_rows % span)[None, :]
    doc_all = jnp.take_along_axis(doc_ids, place_all, axis=1)
    live_all = jnp.take_along_axis(valid, place_all, axis=1)
    doc_own = jnp.take_along_axis(doc_ids, place_own, axis=1)
    cosine, sine = rope_tables(place_own, head_size)
    input_rows = tokens.astype(jnp.float32).reshape(flat_rows, model_width)
    scale_attn = lax.rsqrt(jnp.mean(input_rows * input_rows, axis=-1, keepdims=True) + norm_eps)
    unit_attn = input_rows * scale_attn
    normed_attn = (unit_attn * gain_attn).astype(jnp.bfloat16)

    def project(weight_matrix):
        return jnp.dot(normed_attn, weight_matrix, preferred_element_type=jnp.float32).reshape(
            seq_count, row_count, local_heads, head_size
        )

    query_rot = (
        rotate(project(w_query), cosine, sine, True)
        .astype(jnp.bfloat16)
        .reshape(seq_count, row_count, local_width)
    )
    key_rot = (
        rotate(project(w_key), cosine, sine, True)
        .astype(jnp.bfloat16)
        .reshape(seq_count, row_count, local_width)
    )
    value_low = (
        jnp.dot(normed_attn, w_value, preferred_element_type=jnp.float32)
        .astype(jnp.bfloat16)
        .reshape(seq_count, row_count, local_width)
    )
    key_all, value_all = (
        lax.all_gather(key_rot, "seq", axis=1, tiled=True),
        lax.all_gather(value_low, "seq", axis=1, tiled=True),
    )

    def attend(items):
        query_seq, key_seq, value_seq, place_q, doc_q, place_k, doc_k, live_k = items
        query_heads = query_seq.reshape(row_count, local_heads, head_size)
        key_heads = key_seq.reshape(length, local_heads, head_size)
        value_heads = value_seq.reshape(length, local_heads, head_size)
        mask = visible(place_q, doc_q, place_k, doc_k, live_k)
        weights = (
            jax.nn.sigmoid(score_block(query_heads, key_heads, head_size, length)) * mask
        ).astype(jnp.bfloat16)
        mixed = jnp.einsum("hqk,khe->qhe", weights, value_heads, preferred_element_type=jnp.float32)
        return mixed.astype(jnp.bfloat16).reshape(row_count, local_width)

    attention_output = lax.map(
        attend, (query_rot, key_all, value_all, place_own, doc_own, place_all, doc_all, live_all)
    )
    attended_flat = attention_output.reshape(flat_rows, local_width)
    branch_attn = lax.psum(jnp.dot(attended_flat, w_out, preferred_element_type=jnp.float32), "tp")
    hidden_rows = input_rows + branch_attn
    scale_ffn = lax.rsqrt(jnp.mean(hidden_rows * hidden_rows, axis=-1, keepdims=True) + norm_eps)
    unit_ffn = hidden_rows * scale_ffn
    normalized_feedforward = (unit_ffn * gain_ffn).astype(jnp.bfloat16)
    gate_rows = jnp.dot(normalized_feedforward, w_gate, preferred_element_type=jnp.float32)
    up_projected = jnp.dot(normalized_feedforward, w_up, preferred_element_type=jnp.float32)
    gate_sig = jax.nn.sigmoid(gate_rows)
    activation_rows = (gate_rows * gate_sig * up_projected).astype(jnp.bfloat16)
    branch_ffn = lax.psum(
        jnp.dot(activation_rows, w_down, preferred_element_type=jnp.float32).astype(jnp.bfloat16),
        "tp",
    ).astype(jnp.float32)
    layer_out = (
        (hidden_rows + branch_ffn).astype(jnp.bfloat16).reshape(seq_count, row_count, model_width)
    )
    upstream = cotangent.astype(jnp.float32).reshape(flat_rows, model_width)
    upstream_low = upstream.astype(jnp.bfloat16)
    grad_down = jnp.einsum(
        "tf,td->fd", activation_rows, upstream_low, preferred_element_type=jnp.float32
    )
    grad_act = jnp.einsum("td,fd->tf", upstream_low, w_down, preferred_element_type=jnp.float32)
    gate_pre = (grad_act * up_projected * (gate_sig * (1.0 + gate_rows * (1.0 - gate_sig)))).astype(
        jnp.bfloat16
    )
    up_pre = (grad_act * (gate_rows * gate_sig)).astype(jnp.bfloat16)
    grad_gate = jnp.einsum(
        "td,tf->df", normalized_feedforward, gate_pre, preferred_element_type=jnp.float32
    )
    grad_up = jnp.einsum(
        "td,tf->df", normalized_feedforward, up_pre, preferred_element_type=jnp.float32
    )
    normed_ffn_part = jnp.einsum(
        "tf,df->td", gate_pre, w_gate, preferred_element_type=jnp.float32
    ) + jnp.einsum("tf,df->td", up_pre, w_up, preferred_element_type=jnp.float32)
    grad_normed_ffn = lax.psum(normed_ffn_part, "tp")
    gain_ffn_part = jnp.sum(grad_normed_ffn * unit_ffn, axis=0)
    back_ffn = grad_normed_ffn * gain_ffn
    grad_middle = upstream + scale_ffn * (
        back_ffn - unit_ffn * jnp.mean(back_ffn * unit_ffn, axis=-1, keepdims=True)
    )
    middle_low = grad_middle.astype(jnp.bfloat16)
    grad_out = jnp.einsum(
        "te,td->ed", attended_flat, middle_low, preferred_element_type=jnp.float32
    )
    grad_attended = (
        jnp.einsum("td,ed->te", middle_low, w_out, preferred_element_type=jnp.float32)
        .astype(jnp.bfloat16)
        .reshape(seq_count, row_count, local_width)
    )
    key_back, value_back = (key_all, value_all)

    def attend_back(items):
        query_seq, key_seq, value_seq, grad_seq, place_q, doc_q, place_k, doc_k, live_k = items
        query_heads = query_seq.reshape(row_count, local_heads, head_size)
        key_heads = key_seq.reshape(length, local_heads, head_size)
        value_heads = value_seq.reshape(length, local_heads, head_size)
        grad_heads = grad_seq.reshape(row_count, local_heads, head_size)
        mask = visible(place_q, doc_q, place_k, doc_k, live_k)
        weights, grad_scores = score_grads(
            query_heads, key_heads, value_heads, grad_heads, mask, head_size, length
        )
        grad_value_seq = jnp.einsum(
            "hqk,qhe->khe", weights, grad_heads, preferred_element_type=jnp.float32
        )
        grad_query_seq = (
            jnp.einsum("hqk,khe->qhe", grad_scores, key_heads, preferred_element_type=jnp.float32)
            * factor
        )
        grad_key_seq = (
            jnp.einsum("hqk,qhe->khe", grad_scores, query_heads, preferred_element_type=jnp.float32)
            * factor
        )
        return (
            grad_query_seq,
            grad_key_seq.reshape(length, local_width),
            grad_value_seq.reshape(length, local_width),
        )

    grad_query_rot, grad_key_all, grad_value_all = lax.map(
        attend_back,
        (
            query_rot,
            key_back,
            value_back,
            grad_attended,
            place_own,
            doc_own,
            place_all,
            doc_all,
            live_all,
        ),
    )
    grad_key_rot, grad_value_own = (
        lax.psum_scatter(grad_key_all, "seq", scatter_dimension=1, tiled=True),
        lax.psum_scatter(grad_value_all, "seq", scatter_dimension=1, tiled=True),
    )
    query_low = (
        rotate(grad_query_rot, cosine, sine, False)
        .astype(jnp.bfloat16)
        .reshape(flat_rows, local_width)
    )
    key_low = (
        rotate(
            grad_key_rot.reshape(seq_count, row_count, local_heads, head_size), cosine, sine, False
        )
        .astype(jnp.bfloat16)
        .reshape(flat_rows, local_width)
    )
    value_grad_low = grad_value_own.astype(jnp.bfloat16).reshape(flat_rows, local_width)
    grad_query = jnp.einsum("td,te->de", normed_attn, query_low, preferred_element_type=jnp.float32)
    grad_key = jnp.einsum("td,te->de", normed_attn, key_low, preferred_element_type=jnp.float32)
    grad_value = jnp.einsum(
        "td,te->de", normed_attn, value_grad_low, preferred_element_type=jnp.float32
    )
    normed_attn_part = (
        jnp.einsum("te,de->td", query_low, w_query, preferred_element_type=jnp.float32)
        + jnp.einsum("te,de->td", key_low, w_key, preferred_element_type=jnp.float32)
        + jnp.einsum("te,de->td", value_grad_low, w_value, preferred_element_type=jnp.float32)
    )
    grad_normed_attn = lax.psum(normed_attn_part, "tp")
    gain_attn_part = jnp.sum(grad_normed_attn * unit_attn, axis=0)
    back_attn = grad_normed_attn * gain_attn
    grad_inputs = grad_middle + scale_attn * (
        back_attn - unit_attn * jnp.mean(back_attn * unit_attn, axis=-1, keepdims=True)
    )
    grad_tokens = grad_inputs.reshape(seq_count, row_count, model_width)
    (
        query_shard,
        key_shard,
        value_shard,
        out_shard,
        gain_attn_shard,
        gate_shard,
        up_shard,
        down_shard,
        gain_ffn_shard,
    ) = (
        lax.psum_scatter(grad_query, "seq", scatter_dimension=0, tiled=True),
        lax.psum_scatter(grad_key, "seq", scatter_dimension=0, tiled=True),
        lax.psum_scatter(grad_value, "seq", scatter_dimension=0, tiled=True),
        lax.psum_scatter(grad_out, "seq", scatter_dimension=1, tiled=True),
        lax.psum_scatter(gain_attn_part, "seq", scatter_dimension=0, tiled=True),
        lax.psum_scatter(grad_gate, "seq", scatter_dimension=0, tiled=True),
        lax.psum_scatter(grad_up, "seq", scatter_dimension=0, tiled=True),
        lax.psum_scatter(grad_down, "seq", scatter_dimension=1, tiled=True),
        lax.psum_scatter(gain_ffn_part, "seq", scatter_dimension=0, tiled=True),
    )
    return (
        layer_out,
        grad_tokens,
        gain_attn_shard,
        query_shard,
        key_shard,
        value_shard,
        out_shard,
        gain_ffn_shard,
        gate_shard,
        up_shard,
        down_shard,
    )


def solution(mesh):
    placed = (
        P(None, "seq", None),
        P(),
        P(None, "tp"),
        P(None, "tp"),
        P(None, "tp"),
        P("tp", None),
        P(),
        P(None, "tp"),
        P(None, "tp"),
        P("tp", None),
        P(None, "seq", None),
        P(),
        P(),
        P(),
    )
    return jax.shard_map(
        local,
        mesh=mesh,
        in_specs=placed,
        out_specs=(
            P(None, "seq", None),
            P(None, "seq", None),
            P("seq"),
            P("seq", "tp"),
            P("seq", "tp"),
            P("seq", "tp"),
            P("tp", "seq"),
            P("seq"),
            P("seq", "tp"),
            P("seq", "tp"),
            P("tp", "seq"),
        ),
        check_vma=False,
    )
```

profile of v0, /device:TPU:0, one launch (start us, length us, event | category | flops | bytes accessed | tf_op | source)
XLA Modules:
  0.0 1533.5 jit_solution(12664565859678444474)
XLA Ops:
  9.4 4.4 compare_select_fusion.12
  13.8 5.7 select_select_fusion.1
  25.1 3.9 copy.49
  29.0 3.9 copy.50
  32.9 3.7 fusion.46
  40.6 4.3 fusion.53
  44.9 4.4 compare_select_fusion.3
  50.1 5.7 fusion.75
  55.9 23.0 %gather_fusion.1 = s32[4096]{0:T(1024)S(1)} fusion(s32[4096]{0:T(1024)S(1)} %bitcast.181, s32[4096]{0:T(1024)S(1)} %broadcast_clamp_fusion), kind=kCustom, calls=%fused_computation.clone | custom fusion | bytes 49152 | tf_op jit(solution)/shard_map/jit(take_along_axis)/gather | solution.py:86
  79.0 23.0 %gather_fusion.2 = s32[4096]{0:T(1024)S(1)} fusion(s32[4096]{0:T(1024)S(1)} %bitcast.182, s32[4096]{0:T(1024)S(1)} %broadcast_clamp_fusion), kind=kCustom, calls=%fused_computation.1.clone | custom fusion | bytes 49152 | tf_op jit(solution)/shard_map/jit(take_along_axis)/gather | solution.py:87
  102.2 4.3 and_convert_fusion
  106.5 17.4 %add_divide_fusion = f32[4,512,4096]{2,1,0:T(8,128)} fusion(bf16[4096,4,128]{0,2,1:T(8,128)(2,1)} %bitcast.193, bf16[512,4,64]{0,2,1:T(8,128)(2,1)S(1)} %get-tuple-element.103, bf16[512,4,64]{0,2,1:T(8,128)(2,1)S(1)} %get-tuple-element.102), kind=kOutput, calls=%fused_computation.8 | convolution fusion | flops 2190475264 | bytes 38273024 | tf_op jit(solution)/shard_map/while/body/eval_jaxpr/qhe,khe->hqk/dot_general | solution.py:44
  124.0 16.5 %fusion.56 = bf16[4,128,512]{2,1,0:T(8,128)(2,1)S(1)} fusion(f32[4,512,4096]{2,1,0:T(8,128)} %add_divide_fusion, f32[512,4096]{1,0:T(8,128)} %and_convert_fusion, bf16[4096,512]{1,0:T(8,128)(2,1)} %all-gather.6.cloned.1.call-done), kind=kOutput, calls=%fused_computation.74 | convolution fusion | flops 2164523008 | bytes 46661632 | tf_op jit(solution)/shard_map/while/body/eval_jaxpr/hqk,khe->qhe/dot_general | solution.py:129
  145.2 157.1 %all-reduce.8.cloned.1.call-done = f32[512,2048]{1,0:T(8,128)} async-done(((f32[512,2048]{1,0:T(8,128)}), f32[512,2048]{1,0:T(8,128)}) %all-reduce.8.cloned.1.call-update) | async-done | bytes 4194320 | tf_op jit(solution)/shard_map/psum | solution.py:136
  302.3 3.5 multiply_reduce_fusion.2
  306.2 11.8 fusion.96
  318.1 6.2 fusion.97
  324.3 11.6 multiply_convert_fusion.1
  335.9 8.5 fusion.98
  344.4 9.5 convolution_add_fusion
  354.2 9.8 convolution_convert_fusion
  364.1 144.0 %all-reduce.12.cloned.1.call-done = f32[512,2048]{1,0:T(8,128)} async-done(((f32[512,2048]{1,0:T(8,128)}), f32[512,2048]{1,0:T(8,128)}) %all-reduce.12.cloned.1.call-update) | async-done | bytes 4194320 | tf_op jit(solution)/shard_map/psum | solution.py:171
  508.1 4.4 multiply_reduce_fusion
  512.6 83.9 %all-reduce.10.cloned.1.call-done = bf16[512,2048]{1,0:T(8,128)(2,1)} async-done(((bf16[512,2048]{1,0:T(8,128)(2,1)}), bf16[512,2048]{1,0:T(8,128)(2,1)}) %all-reduce.10.cloned.1.call-update) | async-done | bytes 2097168 | tf_op jit(solution)/shard_map/psum | solution.py:145
  596.4 6.6 multiply_add_fusion
  606.3 21.1 %fusion.2 = bf16[4,512,4096]{2,1,0:T(8,128)(2,1)} fusion(f32[4,512,4096]{2,1,0:T(8,128)} %add_divide_fusion, f32[512,4096]{1,0:T(8,128)} %and_convert_fusion, bf16[512,4,128]{0,2,1:T(8,128)(2,1)S(1)} %bitcast.195, bf16[4096,512]{1,0:T(8,128)(2,1)} %all-gather.6.cloned.1.call-done), kind=kOutput, calls=%fused_computation.6 | convolution fusion | flops 2189426688 | bytes 63438848 | tf_op jit(solution)/shard_map/while/body/eval_jaxpr/qhe,khe->hqk/dot_general | solution.py:51
  627.4 11.4 convolution_multiply_fusion
  639.0 21.6 %fusion.26 = f32[4,128,4096]{2,1,0:T(8,128)} fusion(bf16[512,4,128]{0,2,1:T(8,128)(2,1)S(1)} %bitcast.196, f32[4,512,4096]{2,1,0:T(8,128)} %add_divide_fusion, f32[512,4096]{1,0:T(8,128)} %and_convert_fusion), kind=kOutput, calls=%fused_computation.49 | convolution fusion | flops 2164260864 | bytes 50855936 | tf_op jit(solution)/shard_map/while/body/eval_jaxpr/hqk,qhe->khe/dot_general | solution.py:198
  660.8 13.5 fusion.52
  674.3 35.0 %reduce-scatter.10.cloned.1.call-done = f32[1,512,512]{1,2,0:T(8,128)} async-done(((f32[1,4096,512]{1,2,0:T(8,128)}), f32[1,512,512]{1,2,0:T(8,128)}) %reduce-scatter.10.cloned.1.call-update) | async-done | bytes 1048592 | tf_op jit(solution)/shard_map/reduce_scatter | solution.py:230
  717.4 66.6 %reduce-scatter.12.cloned.1.call-done = f32[1,512,512]{1,2,0:T(8,128)} async-done(((f32[1,4096,512]{1,2,0:T(8,128)}), f32[1,512,512]{1,2,0:T(8,128)}) %reduce-scatter.12.cloned.1.call-update) | async-done | bytes 1048592 | tf_op jit(solution)/shard_map/reduce_scatter | solution.py:231
  784.0 7.0 add_add_fusion
  792.1 5.6 fusion.59
  799.3 4.6 fusion.40
  804.4 3.5 fusion.42
  811.4 12.6 fusion.101
  824.1 12.6 fusion.102
  836.9 12.5 fusion.30
  851.3 94.9 %all-reduce.14.cloned.1.call-done = f32[512,2048]{1,0:T(8,128)} async-done(((f32[512,2048]{1,0:T(8,128)}), f32[512,2048]{1,0:T(8,128)}) %all-reduce.14.cloned.1.call-update) | async-done | bytes 4194320 | tf_op jit(solution)/shard_map/psum | solution.py:256
  949.4 24.0 %all-reduce.2 = (f32[2048]{0:T(1024)S(1)}, f32[2048]{0:T(1024)S(1)}) all-reduce(f32[2048]{0:T(1024)S(1)} %get-tuple-element.70, f32[2048]{0:T(1024)S(1)} %get-tuple-element.68), channel_id=5, replica_groups=mesh['seq'=8,'tp'=4] {'seq'}, use_global_device_ids=true, to_apply=%region_11.13.clone | all-reduce | flops 4096 | bytes 32768
  974.7 7.4 fusion.15
  982.1 18.4 %reduce-scatter.20.cloned.1.call-done = f32[512,256]{1,0:T(8,128)} async-done(((f32[512,2048]{1,0:T(8,128)}), f32[512,256]{1,0:T(8,128)}) %reduce-scatter.20.cloned.1.call-update) | async-done | bytes 524304 | tf_op jit(solution)/shard_map/reduce_scatter | solution.py:277
  1000.5 55.5 %reduce-scatter.18.cloned.1.call-done = f32[256,512]{1,0:T(8,128)} async-done(((f32[2048,512]{1,0:T(8,128)}), f32[256,512]{1,0:T(8,128)}) %reduce-scatter.18.cloned.1.call-update) | async-done | bytes 524304 | tf_op jit(solution)/shard_map/reduce_scatter | solution.py:276
  1056.0 55.3 %reduce-scatter.16.cloned.1.call-done = f32[256,512]{1,0:T(8,128)} async-done(((f32[2048,512]{1,0:T(8,128)}), f32[256,512]{1,0:T(8,128)}) %reduce-scatter.16.cloned.1.call-update) | async-done | bytes 524304 | tf_op jit(solution)/shard_map/reduce_scatter | solution.py:275
  1111.2 55.5 %reduce-scatter.14.cloned.1.call-done = f32[256,512]{1,0:T(8,128)} async-done(((f32[2048,512]{1,0:T(8,128)}), f32[256,512]{1,0:T(8,128)}) %reduce-scatter.14.cloned.1.call-update) | async-done | bytes 524304 | tf_op jit(solution)/shard_map/reduce_scatter | solution.py:274
  1166.8 120.1 %reduce-scatter.22.cloned.1.call-done = f32[256,2048]{1,0:T(8,128)} async-done(((f32[2048,2048]{1,0:T(8,128)}), f32[256,2048]{1,0:T(8,128)}) %reduce-scatter.22.cloned.1.call-update) | async-done | bytes 2097168 | tf_op jit(solution)/shard_map/reduce_scatter | solution.py:279
  1286.9 120.0 %reduce-scatter.24.cloned.1.call-done = f32[256,2048]{1,0:T(8,128)} async-done(((f32[2048,2048]{1,0:T(8,128)}), f32[256,2048]{1,0:T(8,128)}) %reduce-scatter.24.cloned.1.call-update) | async-done | bytes 2097168 | tf_op jit(solution)/shard_map/reduce_scatter | solution.py:280
  1406.9 120.0 %reduce-scatter.26.cloned.1.call-done = f32[2048,256]{1,0:T(8,128)} async-done(((f32[2048,2048]{1,0:T(8,128)}), f32[2048,256]{1,0:T(8,128)}) %reduce-scatter.26.cloned.1.call-update) | async-done | bytes 2097168 | tf_op jit(solution)/shard_map/reduce_scatter | solution.py:281
  (140 shorter events, 42.5 us)
Async XLA Ops:
  7.2 134.1 %copy-start = (bf16[512,2048]{1,0:T(8,128)(2,1)S(1)}, bf16[512,2048]{1,0:T(8,128)(2,1)}, u32[]{:S(2)}) copy-start(bf16[512,2048]{1,0:T(8,128)(2,1)} %param.21) | copy-start | bytes 6291460
  7.2 99.3 %all-gather.4.cloned.1.call-start = ((), (), s32[]{:S(2)}) async-start(), calls=%async_computation.9 | async-start | bytes 4718592 | tf_op jit(solution)/shard_map/all_gather | solution.py:116
  25.0 15.5 %copy-start.22 = (f32[512]{0:T(512)}, f32[512]{0:T(512)S(1)}, u32[]{:S(2)}) copy-start(f32[512]{0:T(512)S(1)} %add_rsqrt_fusion.1) | copy-start | bytes 6148
  25.1 7.8 copy-start.20
  32.9 3.7 copy-start.4
  32.9 3.8 copy-start.15
  38.6 0.7 copy-start.16
  38.6 1.0 copy-start.18
  40.5 15.4 %copy-start.2 = (s32[1,4096]{1,0:T(1,128)S(1)}, s32[1,4096]{1,0:T(1,128)}, u32[]{:S(2)}) copy-start(s32[1,4096]{1,0:T(1,128)} %param.27) | copy-start | bytes 49156
  40.5 83.5 %all-gather.6.cloned.1.call-start = ((), (), s32[]{:S(2)}) async-start(), calls=%async_computation.23 | async-start | bytes 4718592 | tf_op jit(solution)/shard_map/all_gather | solution.py:117
  44.9 257.4 %all-reduce.8.cloned.1.call-start = ((), (), s32[]{:S(2)}) async-start(), calls=%async_computation.10 | async-start | bytes 8388608 | tf_op jit(solution)/shard_map/psum | solution.py:136
  55.9 23.1 %copy-start.3 = (s32[1,4096]{1,0:T(1,128)S(1)}, s32[1,4096]{1,0:T(1,128)}, u32[]{:S(2)}) copy-start(s32[1,4096]{1,0:T(1,128)} %param.28) | copy-start | bytes 49156
  140.5 0.8 copy-start.10
  144.6 161.2 %copy-start.24 = (f32[2048]{0:T(1024)S(1)}, f32[2048]{0:T(1024)}, u32[]{:S(2)}) copy-start(f32[2048]{0:T(1024)} %param.22) | copy-start | bytes 24580
  144.6 363.5 %all-reduce.12.cloned.1.call-start = ((), (), s32[]{:S(2)}) async-start(), calls=%async_computation.12 | async-start | bytes 8388608 | tf_op jit(solution)/shard_map/psum | solution.py:171
  305.7 12.3 copy-start.6
  305.8 12.3 slice-start
  306.2 11.9 copy-start.14
  306.2 11.9 slice-start.1
  318.1 6.2 copy-start.13
  335.9 8.5 copy-start.27
  335.9 8.5 copy-start.26
  354.0 242.5 %all-reduce.10.cloned.1.call-start = ((), (), s32[]{:S(2)}) async-start(), calls=%async_computation.11 | async-start | bytes 4194304 | tf_op jit(solution)/shard_map/psum | solution.py:145
  364.0 345.2 %reduce-scatter.10.cloned.1.call-start = ((), (), s32[]{:S(2)}) async-start(), calls=%async_computation.13 | async-start | bytes 9437184 | tf_op jit(solution)/shard_map/reduce_scatter | solution.py:230
  603.0 2.0 copy-start.7
  638.9 145.1 %reduce-scatter.12.cloned.1.call-start = ((), (), s32[]{:S(2)}) async-start(), calls=%async_computation.14 | async-start | bytes 9437184 | tf_op jit(solution)/shard_map/reduce_scatter | solution.py:231
  660.5 48.7 %copy-start.17 = (f32[512,64]{0,1:T(8,128)S(1)}, f32[512,64]{0,1:T(8,128)}, u32[]{:S(2)}) copy-start(f32[512,64]{0,1:T(8,128)} %copy-done.16) | copy-start | bytes 393220
  660.5 48.7 %copy-start.19 = (f32[512,64]{0,1:T(8,128)S(1)}, f32[512,64]{0,1:T(8,128)}, u32[]{:S(2)}) copy-start(f32[512,64]{0,1:T(8,128)} %copy-done.18) | copy-start | bytes 393220
  660.6 285.6 %all-reduce.14.cloned.1.call-start = ((), (), s32[]{:S(2)}) async-start(), calls=%async_computation.15 | async-start | bytes 8388608 | tf_op jit(solution)/shard_map/psum | solution.py:256
  674.3 36.6 %copy-start.8 = (bf16[2048,512]{1,0:T(8,128)(2,1)S(1)}, bf16[2048,512]{1,0:T(8,128)(2,1)}, u32[]{:S(2)}) copy-start(bf16[2048,512]{1,0:T(8,128)(2,1)} %param.19) | copy-start | bytes 6291460
  710.9 3.3 copy-start.9
  714.2 69.9 %copy-start.12 = (bf16[2048,512]{1,0:T(8,128)(2,1)S(1)}, bf16[2048,512]{1,0:T(8,128)(2,1)}, u32[]{:S(2)}) copy-start(bf16[2048,512]{1,0:T(8,128)(2,1)} %param.20) | copy-start | bytes 6291460
  791.0 1.0 copy-start.11
  791.0 209.4 %reduce-scatter.20.cloned.1.call-start = ((), (), s32[]{:S(2)}) async-start(), calls=%async_computation.19 | async-start | bytes 4718592 | tf_op jit(solution)/shard_map/reduce_scatter | solution.py:277
  797.7 1.6 copy-start.5
  797.7 1.6 copy-start.21
  797.7 1.6 copy-start.23
  797.7 258.3 %reduce-scatter.18.cloned.1.call-start = ((), (), s32[]{:S(2)}) async-start(), calls=%async_computation.18 | async-start | bytes 4718592 | tf_op jit(solution)/shard_map/reduce_scatter | solution.py:276
  803.9 307.3 %reduce-scatter.16.cloned.1.call-start = ((), (), s32[]{:S(2)}) async-start(), calls=%async_computation.17 | async-start | bytes 4718592 | tf_op jit(solution)/shard_map/reduce_scatter | solution.py:275
  807.9 358.9 %reduce-scatter.14.cloned.1.call-start = ((), (), s32[]{:S(2)}) async-start(), calls=%async_computation.16 | async-start | bytes 4718592 | tf_op jit(solution)/shard_map/reduce_scatter | solution.py:274
  811.3 475.5 %reduce-scatter.22.cloned.1.call-start = ((), (), s32[]{:S(2)}) async-start(), calls=%async_computation.20 | async-start | bytes 18874368 | tf_op jit(solution)/shard_map/reduce_scatter | solution.py:279
  824.0 582.8 %reduce-scatter.24.cloned.1.call-start = ((), (), s32[]{:S(2)}) async-start(), calls=%async_computation.21 | async-start | bytes 18874368 | tf_op jit(solution)/shard_map/reduce_scatter | solution.py:280
  836.6 690.2 %reduce-scatter.26.cloned.1.call-start = ((), (), s32[]{:S(2)}) async-start(), calls=%async_computation.22 | async-start | bytes 18874368 | tf_op jit(solution)/shard_map/reduce_scatter | solution.py:281
  849.4 0.7 copy-start.25
  974.7 552.1 %copy-start.1 = (bf16[512,2048]{1,0:T(8,128)(2,1)S(1)}, bf16[512,2048]{1,0:T(8,128)(2,1)}, u32[]{:S(2)}) copy-start(bf16[512,2048]{1,0:T(8,128)(2,1)} %param.21) | copy-start | bytes 6291460
Sparse Core Ops, SparseCore 0:
  40.6 40.1 all-gather.3
  83.2 36.7 all-gather.5
  144.7 157.5 all-reduce.7
  354.1 153.9 all-reduce.11
  510.9 85.5 all-reduce.9
  639.0 70.1 reduce-scatter.9
  712.7 71.2 reduce-scatter.11
  791.2 154.9 all-reduce.13
  950.1 50.3 reduce-scatter.19
  1004.6 51.2 reduce-scatter.17
  1059.9 51.2 reduce-scatter.15
  1115.4 51.3 reduce-scatter.13
  1170.9 115.9 reduce-scatter.21
  1290.9 115.9 reduce-scatter.23
  1410.8 115.9 reduce-scatter.25
where the time goes:
time: 1540 us; the launch traced here: 1530 us
  waiting for transfers between devices  1130 us (73%)
  matrix products  241 us (16%)
  local copies, waits for them, and re-layouts  67.8 us (4%)
  other arithmetic  56.7 us (4%)
  blocking collectives  24 us (2%)
    psum x1, waiting for transfers between devices, local(): lax.psum(jnp.dot(attended_flat, w_out, preferred_element_type=jnp.float32...  157 us
    psum x1, waiting for transfers between devices, local(): grad_normed_ffn = lax.psum(normed_ffn_part, 'tp')  144 us
    reduce_scatter x1, waiting for transfers between devices, local(): lax.psum_scatter(grad_gate, 'seq', scatter_dimension=0, tiled=True)  120 us
    reduce_scatter x1, waiting for transfers between devices, local(): lax.psum_scatter(grad_up, 'seq', scatter_dimension=0, tiled=True)  120 us
    reduce_scatter x1, waiting for transfers between devices, local(): lax.psum_scatter(grad_down, 'seq', scatter_dimension=1, tiled=True)  120 us
    psum x1, waiting for transfers between devices, local(): grad_normed_attn = lax.psum(normed_attn_part, 'tp')  94.9 us
    psum x1, waiting for transfers between devices, local(): lax.psum(jnp.dot(activation_rows, w_down, preferred_element_type=jnp.floa...  83.9 us
    reduce_scatter x1, waiting for transfers between devices, local(): lax.psum_scatter(grad_value_all, 'seq', scatter_dimension=1, tiled=True)  66.6 us
  transfers between devices with their start and end apart: 15, of which 13 were waited for; matrix products, arithmetic and copies ran while one was open for 14% of the time, Pallas kernels for 0%

commit v1 on v0

--- a/solution.py
+++ b/solution.py
@@ -7,6 +7,11 @@
 HEAD_WIDTH = 128
 norm_eps = 1e-05
 rope_base = 10000.0
+
+
+def summed_here(value, name):
+    parts = lax.all_gather(value, name)
+    return jnp.sum(parts, axis=0)
 
 
 def rope_tables(places, head_size):
@@ -142,7 +147,7 @@
     up_projected = jnp.dot(normalized_feedforward, w_up, preferred_element_type=jnp.float32)
     gate_sig = jax.nn.sigmoid(gate_rows)
     activation_rows = (gate_rows * gate_sig * up_projected).astype(jnp.bfloat16)
-    branch_ffn = lax.psum(
+    branch_ffn = summed_here(
         jnp.dot(activation_rows, w_down, preferred_element_type=jnp.float32).astype(jnp.bfloat16),
         "tp",
     ).astype(jnp.float32)

time: 1540 us -> 1610 us (1.045)
  waiting for transfers between devices: 1130 us -> 1190 us
    all_gather x0 -> x1, waiting for transfers between devices: none -> 146 us  [summed_here(): parts = lax.all_gather(value, name)]
    psum x1 -> x0, waiting for transfers between devices: 83.9 us -> none  [local(): lax.psum(jnp.dot(activation_rows, w_down, preferred_element_type=jnp.floa...]
  transfers between devices with their start and end apart: 15 -> 15, of which waited for: 13 -> 13; matrix products, arithmetic and copies ran while one was open for 14% -> 12% of each run, Pallas kernels for 0% -> 0%
where the time goes in v1:
time: 1610 us; the launch traced here: 1600 us
  waiting for transfers between devices  1190 us (74%)
  matrix products  233 us (14%)
  local copies, waits for them, and re-layouts  70.9 us (4%)
  other arithmetic  64 us (4%)
  blocking collectives  24 us (1%)
    psum x1, waiting for transfers between devices, local(): lax.psum(jnp.dot(attended_flat, w_out, preferred_element_type=jnp.float32...  158 us
    all_gather x1, waiting for transfers between devices, summed_here(): parts = lax.all_gather(value, name)  146 us
    psum x1, waiting for transfers between devices, local(): grad_normed_ffn = lax.psum(normed_ffn_part, 'tp')  144 us
    reduce_scatter x1, waiting for transfers between devices, local(): lax.psum_scatter(grad_up, 'seq', scatter_dimension=0, tiled=True)  120 us
    reduce_scatter x1, waiting for transfers between devices, local(): lax.psum_scatter(grad_down, 'seq', scatter_dimension=1, tiled=True)  120 us
    reduce_scatter x1, waiting for transfers between devices, local(): lax.psum_scatter(grad_gate, 'seq', scatter_dimension=0, tiled=True)  120 us
    psum x1, waiting for transfers between devices, local(): grad_normed_attn = lax.psum(normed_attn_part, 'tp')  101 us
    reduce_scatter x1, waiting for transfers between devices, local(): lax.psum_scatter(grad_value_all, 'seq', scatter_dimension=1, tiled=True)  67 us
  transfers between devices with their start and end apart: 15, of which 13 were waited for; matrix products, arithmetic and copies ran while one was open for 12% of the time, Pallas kernels for 0%

profile of v1, /device:TPU:0, one launch (start us, length us, event | category | flops | bytes accessed | tf_op | source)
XLA Modules:
  0.0 1603.0 jit_solution(7581747670245494147)
XLA Ops:
  9.4 4.4 compare_select_fusion.12
  13.8 5.7 select_select_fusion.1
  25.1 3.9 copy.49
  29.0 3.9 copy.50
  32.9 3.7 fusion.46
  40.6 4.3 fusion.53
  44.9 4.4 compare_select_fusion.3
  50.3 5.7 fusion.75
  56.1 23.0 %gather_fusion.1 = s32[4096]{0:T(1024)S(1)} fusion(s32[4096]{0:T(1024)S(1)} %bitcast.182, s32[4096]{0:T(1024)S(1)} %broadcast_clamp_fusion), kind=kCustom, calls=%fused_computation.clone | custom fusion | bytes 49152 | tf_op jit(solution)/shard_map/jit(take_along_axis)/gather | solution.py:91
  79.1 23.0 %gather_fusion.2 = s32[4096]{0:T(1024)S(1)} fusion(s32[4096]{0:T(1024)S(1)} %bitcast.183, s32[4096]{0:T(1024)S(1)} %broadcast_clamp_fusion), kind=kCustom, calls=%fused_computation.1.clone | custom fusion | bytes 49152 | tf_op jit(solution)/shard_map/jit(take_along_axis)/gather | solution.py:92
  102.3 4.3 and_convert_fusion
  106.7 17.4 %add_divide_fusion = f32[4,512,4096]{2,1,0:T(8,128)} fusion(bf16[4096,4,128]{0,2,1:T(8,128)(2,1)} %bitcast.195, bf16[512,4,64]{0,2,1:T(8,128)(2,1)S(1)} %get-tuple-element.103, bf16[512,4,64]{0,2,1:T(8,128)(2,1)S(1)} %get-tuple-element.102), kind=kOutput, calls=%fused_computation.8 | convolution fusion | flops 2190475264 | bytes 38273024 | tf_op jit(solution)/shard_map/while/body/eval_jaxpr/qhe,khe->hqk/dot_general | solution.py:49
  124.1 16.5 %fusion.56 = bf16[4,128,512]{2,1,0:T(8,128)(2,1)S(1)} fusion(f32[4,512,4096]{2,1,0:T(8,128)} %add_divide_fusion, f32[512,4096]{1,0:T(8,128)} %and_convert_fusion, bf16[4096,512]{1,0:T(8,128)(2,1)} %all-gather.8.cloned.1.call-done), kind=kOutput, calls=%fused_computation.74 | convolution fusion | flops 2164523008 | bytes 46661632 | tf_op jit(solution)/shard_map/while/body/eval_jaxpr/hqk,khe->qhe/dot_general | solution.py:134
  145.0 157.5 %all-reduce.7.cloned.1.call-done = f32[512,2048]{1,0:T(8,128)} async-done(((f32[512,2048]{1,0:T(8,128)}), f32[512,2048]{1,0:T(8,128)}) %all-reduce.7.cloned.1.call-update) | async-done | bytes 4194320 | tf_op jit(solution)/shard_map/psum | solution.py:141
  302.5 3.5 multiply_reduce_fusion.2
  306.5 11.8 fusion.96
  318.3 6.2 fusion.97
  324.5 11.7 multiply_convert_fusion.1
  336.1 8.5 fusion.98
  344.6 9.5 convolution_add_fusion
  354.7 9.9 convolution_convert_fusion
  364.6 143.7 %all-reduce.9.cloned.1.call-done = f32[512,2048]{1,0:T(8,128)} async-done(((f32[512,2048]{1,0:T(8,128)}), f32[512,2048]{1,0:T(8,128)}) %all-reduce.9.cloned.1.call-update) | async-done | bytes 4194320 | tf_op jit(solution)/shard_map/psum | solution.py:176
  508.3 4.4 multiply_reduce_fusion
  512.8 146.2 %all-gather.10.cloned.1.call-done = bf16[2048,2048]{1,0:T(8,128)(2,1)} async-done(((bf16[512,2048]{1,0:T(8,128)(2,1)}), bf16[2048,2048]{1,0:T(8,128)(2,1)}) %all-gather.10.cloned.1.call-update) | async-done | bytes 8388624 | tf_op jit(solution)/shard_map/all_gather | solution.py:13
  659.0 7.2 reduce_sum.68
  666.2 6.6 multiply_add_fusion
  676.1 21.1 %fusion.2 = bf16[4,512,4096]{2,1,0:T(8,128)(2,1)} fusion(f32[4,512,4096]{2,1,0:T(8,128)} %add_divide_fusion, f32[512,4096]{1,0:T(8,128)} %and_convert_fusion, bf16[512,4,128]{0,2,1:T(8,128)(2,1)S(1)} %bitcast.197, bf16[4096,512]{1,0:T(8,128)(2,1)} %all-gather.8.cloned.1.call-done), kind=kOutput, calls=%fused_computation.6 | convolution fusion | flops 2189426688 | bytes 63438848 | tf_op jit(solution)/shard_map/while/body/eval_jaxpr/qhe,khe->hqk/dot_general | solution.py:56
  697.2 11.5 convolution_multiply_fusion
  708.7 21.6 %fusion.26 = f32[4,128,4096]{2,1,0:T(8,128)} fusion(bf16[512,4,128]{0,2,1:T(8,128)(2,1)S(1)} %bitcast.198, f32[4,512,4096]{2,1,0:T(8,128)} %add_divide_fusion, f32[512,4096]{1,0:T(8,128)} %and_convert_fusion), kind=kOutput, calls=%fused_computation.49 | convolution fusion | flops 2164260864 | bytes 50855936 | tf_op jit(solution)/shard_map/while/body/eval_jaxpr/hqk,qhe->khe/dot_general | solution.py:203
  730.6 13.5 fusion.52
  744.0 34.3 %reduce-scatter.10.cloned.1.call-done = f32[1,512,512]{1,2,0:T(8,128)} async-done(((f32[1,4096,512]{1,2,0:T(8,128)}), f32[1,512,512]{1,2,0:T(8,128)}) %reduce-scatter.10.cloned.1.call-update) | async-done | bytes 1048592 | tf_op jit(solution)/shard_map/reduce_scatter | solution.py:235
  786.4 67.0 %reduce-scatter.12.cloned.1.call-done = f32[1,512,512]{1,2,0:T(8,128)} async-done(((f32[1,4096,512]{1,2,0:T(8,128)}), f32[1,512,512]{1,2,0:T(8,128)}) %reduce-scatter.12.cloned.1.call-update) | async-done | bytes 1048592 | tf_op jit(solution)/shard_map/reduce_scatter | solution.py:236
  853.5 7.0 add_add_fusion
  861.5 5.6 fusion.59
  868.7 9.8 fusion.101
  878.8 9.8 fusion.102
  890.2 9.7 fusion.30
  901.5 4.6 fusion.40
  915.1 100.6 %all-reduce.11.cloned.1.call-done = f32[512,2048]{1,0:T(8,128)} async-done(((f32[512,2048]{1,0:T(8,128)}), f32[512,2048]{1,0:T(8,128)}) %all-reduce.11.cloned.1.call-update) | async-done | bytes 4194320 | tf_op jit(solution)/shard_map/psum | solution.py:261
  1018.9 24.0 %all-reduce.2 = (f32[2048]{0:T(1024)S(1)}, f32[2048]{0:T(1024)S(1)}) all-reduce(f32[2048]{0:T(1024)S(1)} %get-tuple-element.70, f32[2048]{0:T(1024)S(1)} %get-tuple-element.68), channel_id=6, replica_groups=mesh['seq'=8,'tp'=4] {'seq'}, use_global_device_ids=true, to_apply=%region_11.13.clone | all-reduce | flops 4096 | bytes 32768
  1044.2 7.3 fusion.15
  1051.5 18.8 %reduce-scatter.20.cloned.1.call-done = f32[512,256]{1,0:T(8,128)} async-done(((f32[512,2048]{1,0:T(8,128)}), f32[512,256]{1,0:T(8,128)}) %reduce-scatter.20.cloned.1.call-update) | async-done | bytes 524304 | tf_op jit(solution)/shard_map/reduce_scatter | solution.py:282
  1070.3 120.0 %reduce-scatter.22.cloned.1.call-done = f32[256,2048]{1,0:T(8,128)} async-done(((f32[2048,2048]{1,0:T(8,128)}), f32[256,2048]{1,0:T(8,128)}) %reduce-scatter.22.cloned.1.call-update) | async-done | bytes 2097168 | tf_op jit(solution)/shard_map/reduce_scatter | solution.py:284
  1190.2 120.1 %reduce-scatter.24.cloned.1.call-done = f32[256,2048]{1,0:T(8,128)} async-done(((f32[2048,2048]{1,0:T(8,128)}), f32[256,2048]{1,0:T(8,128)}) %reduce-scatter.24.cloned.1.call-update) | async-done | bytes 2097168 | tf_op jit(solution)/shard_map/reduce_scatter | solution.py:285
  1310.4 120.0 %reduce-scatter.26.cloned.1.call-done = f32[2048,256]{1,0:T(8,128)} async-done(((f32[2048,2048]{1,0:T(8,128)}), f32[2048,256]{1,0:T(8,128)}) %reduce-scatter.26.cloned.1.call-update) | async-done | bytes 2097168 | tf_op jit(solution)/shard_map/reduce_scatter | solution.py:286
  1430.3 55.3 %reduce-scatter.18.cloned.1.call-done = f32[256,512]{1,0:T(8,128)} async-done(((f32[2048,512]{1,0:T(8,128)}), f32[256,512]{1,0:T(8,128)}) %reduce-scatter.18.cloned.1.call-update) | async-done | bytes 524304 | tf_op jit(solution)/shard_map/reduce_scatter | solution.py:281
  1485.6 55.5 %reduce-scatter.16.cloned.1.call-done = f32[256,512]{1,0:T(8,128)} async-done(((f32[2048,512]{1,0:T(8,128)}), f32[256,512]{1,0:T(8,128)}) %reduce-scatter.16.cloned.1.call-update) | async-done | bytes 524304 | tf_op jit(solution)/shard_map/reduce_scatter | solution.py:280
  1541.2 55.1 %reduce-scatter.14.cloned.1.call-done = f32[256,512]{1,0:T(8,128)} async-done(((f32[2048,512]{1,0:T(8,128)}), f32[256,512]{1,0:T(8,128)}) %reduce-scatter.14.cloned.1.call-update) | async-done | bytes 524304 | tf_op jit(solution)/shard_map/reduce_scatter | solution.py:279
  (145 shorter events, 48.7 us)
Async XLA Ops:
  7.2 134.3 %copy-start = (bf16[512,2048]{1,0:T(8,128)(2,1)S(1)}, bf16[512,2048]{1,0:T(8,128)(2,1)}, u32[]{:S(2)}) copy-start(bf16[512,2048]{1,0:T(8,128)(2,1)} %param.21) | copy-start | bytes 6291460
  7.2 99.5 %all-gather.6.cloned.1.call-start = ((), (), s32[]{:S(2)}) async-start(), calls=%async_computation.9 | async-start | bytes 4718592 | tf_op jit(solution)/shard_map/all_gather | solution.py:121
  25.0 15.5 copy-start.24
  25.1 7.8 copy-start.22
  32.9 3.7 copy-start.4
  32.9 3.8 copy-start.17
  38.6 0.7 copy-start.18
  38.6 1.0 copy-start.20
  40.5 15.6 copy-start.2
  40.5 83.6 %all-gather.8.cloned.1.call-start = ((), (), s32[]{:S(2)}) async-start(), calls=%async_computation.22 | async-start | bytes 4718592 | tf_op jit(solution)/shard_map/all_gather | solution.py:122
  44.9 257.6 %all-reduce.7.cloned.1.call-start = ((), (), s32[]{:S(2)}) async-start(), calls=%async_computation.10 | async-start | bytes 8388608 | tf_op jit(solution)/shard_map/psum | solution.py:141
  56.1 23.1 %copy-start.3 = (s32[1,4096]{1,0:T(1,128)S(1)}, s32[1,4096]{1,0:T(1,128)}, u32[]{:S(2)}) copy-start(s32[1,4096]{1,0:T(1,128)} %param.28) | copy-start | bytes 49156
  140.6 0.8 copy-start.10
  144.7 161.3 %copy-start.26 = (f32[2048]{0:T(1024)S(1)}, f32[2048]{0:T(1024)}, u32[]{:S(2)}) copy-start(f32[2048]{0:T(1024)} %param.22) | copy-start | bytes 24580
  144.8 363.6 %all-reduce.9.cloned.1.call-start = ((), (), s32[]{:S(2)}) async-start(), calls=%async_computation.11 | async-start | bytes 8388608 | tf_op jit(solution)/shard_map/psum | solution.py:176
  306.0 12.3 copy-start.6
  306.0 12.3 slice-start
  306.4 11.9 copy-start.15
  306.5 11.9 slice-start.1
  318.3 6.2 copy-start.13
  336.1 8.5 copy-start.29
  336.1 8.5 copy-start.28
  354.2 304.8 %all-gather.10.cloned.1.call-start = ((), (), s32[]{:S(2)}) async-start(), calls=%async_computation.23 | async-start | bytes 10485760 | tf_op jit(solution)/shard_map/all_gather | solution.py:13
  364.5 413.8 %reduce-scatter.10.cloned.1.call-start = ((), (), s32[]{:S(2)}) async-start(), calls=%async_computation.12 | async-start | bytes 9437184 | tf_op jit(solution)/shard_map/reduce_scatter | solution.py:235
  672.8 2.0 copy-start.7
  708.7 144.8 %reduce-scatter.12.cloned.1.call-start = ((), (), s32[]{:S(2)}) async-start(), calls=%async_computation.13 | async-start | bytes 9437184 | tf_op jit(solution)/shard_map/reduce_scatter | solution.py:236
  730.3 48.0 %copy-start.19 = (f32[512,64]{0,1:T(8,128)S(1)}, f32[512,64]{0,1:T(8,128)}, u32[]{:S(2)}) copy-start(f32[512,64]{0,1:T(8,128)} %copy-done.18) | copy-start | bytes 393220
  730.3 48.0 %copy-start.21 = (f32[512,64]{0,1:T(8,128)S(1)}, f32[512,64]{0,1:T(8,128)}, u32[]{:S(2)}) copy-start(f32[512,64]{0,1:T(8,128)} %copy-done.20) | copy-start | bytes 393220
  730.4 285.3 %all-reduce.11.cloned.1.call-start = ((), (), s32[]{:S(2)}) async-start(), calls=%async_computation.14 | async-start | bytes 8388608 | tf_op jit(solution)/shard_map/psum | solution.py:261
  744.0 35.9 %copy-start.8 = (bf16[2048,512]{1,0:T(8,128)(2,1)S(1)}, bf16[2048,512]{1,0:T(8,128)(2,1)}, u32[]{:S(2)}) copy-start(bf16[2048,512]{1,0:T(8,128)(2,1)} %param.19) | copy-start | bytes 6291460
  779.9 3.2 copy-start.9
  783.2 70.3 %copy-start.12 = (bf16[2048,512]{1,0:T(8,128)(2,1)S(1)}, bf16[2048,512]{1,0:T(8,128)(2,1)}, u32[]{:S(2)}) copy-start(bf16[2048,512]{1,0:T(8,128)(2,1)} %param.20) | copy-start | bytes 6291460
  860.5 1.0 copy-start.11
  860.5 209.8 %reduce-scatter.20.cloned.1.call-start = ((), (), s32[]{:S(2)}) async-start(), calls=%async_computation.18 | async-start | bytes 4718592 | tf_op jit(solution)/shard_map/reduce_scatter | solution.py:282
  867.1 1.6 copy-start.16
  867.1 323.1 %reduce-scatter.22.cloned.1.call-start = ((), (), s32[]{:S(2)}) async-start(), calls=%async_computation.19 | async-start | bytes 18874368 | tf_op jit(solution)/shard_map/reduce_scatter | solution.py:284
  878.5 431.9 %reduce-scatter.24.cloned.1.call-start = ((), (), s32[]{:S(2)}) async-start(), calls=%async_computation.20 | async-start | bytes 18874368 | tf_op jit(solution)/shard_map/reduce_scatter | solution.py:285
  888.6 1.6 copy-start.14
  888.6 541.7 %reduce-scatter.26.cloned.1.call-start = ((), (), s32[]{:S(2)}) async-start(), calls=%async_computation.21 | async-start | bytes 18874368 | tf_op jit(solution)/shard_map/reduce_scatter | solution.py:286
  899.9 1.7 copy-start.5
  899.9 1.7 copy-start.23
  899.9 1.7 copy-start.25
  899.9 585.8 %reduce-scatter.18.cloned.1.call-start = ((), (), s32[]{:S(2)}) async-start(), calls=%async_computation.17 | async-start | bytes 4718592 | tf_op jit(solution)/shard_map/reduce_scatter | solution.py:281
  906.2 635.0 %reduce-scatter.16.cloned.1.call-start = ((), (), s32[]{:S(2)}) async-start(), calls=%async_computation.16 | async-start | bytes 4718592 | tf_op jit(solution)/shard_map/reduce_scatter | solution.py:280
  909.7 686.6 %reduce-scatter.14.cloned.1.call-start = ((), (), s32[]{:S(2)}) async-start(), calls=%async_computation.15 | async-start | bytes 4718592 | tf_op jit(solution)/shard_map/reduce_scatter | solution.py:279
  913.2 0.7 copy-start.27
  1044.2 552.1 %copy-start.1 = (bf16[512,2048]{1,0:T(8,128)(2,1)S(1)}, bf16[512,2048]{1,0:T(8,128)(2,1)}, u32[]{:S(2)}) copy-start(bf16[512,2048]{1,0:T(8,128)(2,1)} %param.21) | copy-start | bytes 6291460
Sparse Core Ops, SparseCore 0:
  40.6 40.1 all-gather.5
  83.2 36.7 all-gather.7
  144.9 157.5 all-reduce.6
  354.3 153.9 all-reduce.8
  510.3 148.6 all-gather.9
  708.8 69.4 reduce-scatter.9
  782.2 71.2 reduce-scatter.11
  860.6 154.9 all-reduce.10
  1019.9 50.3 reduce-scatter.19
  1074.3 115.9 reduce-scatter.21
  1194.4 115.9 reduce-scatter.23
  1314.4 115.9 reduce-scatter.25
  1434.3 51.3 reduce-scatter.17
  1489.8 51.3 reduce-scatter.15
  1544.9 51.2 reduce-scatter.13
